TPU v7x, 256 devices: a whole 4x4x8 slice. The times are simulated.
256 devices in a mesh: row: 32 (over z, y), col: 8 (over x, core).
Axes of the slice: x: 4, y: 4, z: 8, core: 2. Of those that a mesh axis runs over, the one named last changes fastest.
Arguments:
- obstacles: float32 [3, 16384], P(None, 'row'), may hold values from 0 to 16
- particles: float32 [3, 8192], P(None, 'row'), may hold values from 0 to 16
- forces: float32 [3, 32, 8192], P(None, None, 'row'), may hold values from -0.8 to 0.8
- neighbours: int32 [64, 32], P('row', 'col'), may hold values from 0 to 127, as said below
- carried: float32 [128, 3, 32, 128], P('row'), may hold values from -6 to 6
- factor: float32 [2, 4096, 128, 3, 128], P(None, 'col', 'row'), may hold values from -0.09375 to 0.09375
- inverses: float32 [2, 4096, 4096], P(None, 'row', 'col'), may hold values from -0.09375 to 0.09375
Outputs:
- solved: float32 [2, 32, 4096], P(None, None, 'col')
- remaining: float32 [128, 3, 32, 128], P('row', None, 'col')
Inputs may be any that keep to these rules, and one draw needn't show every extreme that they name: `neighbours`: each particle block lists 32 different obstacle blocks, and every obstacle block is listed by exactly 16 particle blocks.
All inputs are finite; a program needn't handle non-finite values.
Results may differ from a plain program's by a relative error of at most 0.0001.
Values sent between devices are 32-bit elements; how exact they have to be, the bound alone decides.
No kernel may reach another device: no remote copies, remote signals or barrier semaphores. Data moves between devices by JAX's collectives and lax.ppermute only.
A program may use at most 64 MiB of HBM per device.

v0:
```python
import jax
import jax.numpy as jnp
from jax import lax
from jax.sharding import PartitionSpec as P

PANEL = 4096
BLOCK_PTS = 128
GROUP = 128
soften_square = 1.0
highest = lax.Precision.HIGHEST


def stokeslet(targets, sources, pushes, weight):
    difference = targets[:, :, None] - sources[:, None, :]
    radius = jnp.sum(difference * difference, axis=0) + soften_square
    inverse_cube = lax.rsqrt(radius) / radius * weight
    isotropic = (radius + soften_square) * inverse_cube
    speeds = []
    for left_comp in range(3):
        summed = jnp.einsum("sq,xq->sx", pushes[left_comp], isotropic, precision=highest)
        for right_comp in range(3):
            coupling = difference[left_comp] * difference[right_comp] * inverse_cube
            summed = summed + jnp.einsum(
                "sq,xq->sx", pushes[right_comp], coupling, precision=highest
            )
        speeds.append(summed)
    return jnp.stack(speeds)


def keep_mask(panel_step, block_count, diag_count):
    component = jnp.arange(3, dtype=jnp.int32)[None, :, None, None]
    position = (
        jnp.arange(block_count, dtype=jnp.int32)[:, None] * BLOCK_PTS
        + jnp.arange(BLOCK_PTS, dtype=jnp.int32)[None, :]
    )
    position = position[:, None, None, :]
    hidden_rows = (component <= panel_step) & (position < diag_count)
    return jnp.where(hidden_rows, 0.0, 1.0).astype(jnp.float32)


def diag_view(values, component, diag_count):
    picked = values[:, component]
    return picked.transpose(1, 0, 2).reshape(picked.shape[1], -1)[:, :diag_count]


def solve_block(diag_rows, inverse):
    partial_rows = jnp.dot(
        diag_rows, inverse, precision=highest, preferred_element_type=jnp.float32
    )
    return lax.psum(partial_rows, "row")


def panel_change(answer, panel_cols):
    return jnp.einsum("sj,jbai->basi", answer, panel_cols, precision=highest)


def body(obstacles, particles, forces, neighbours, carried, factor, inverses):
    row_count = lax.axis_size("row")
    col_count = lax.axis_size("col")
    block_count = obstacles.shape[1] // BLOCK_PTS
    diag_count = PANEL // row_count
    rhs_count = forces.shape[1]
    group_count = particles.shape[1] // GROUP
    rhs_share = rhs_count // col_count
    every_point = lax.all_gather(obstacles, "row", axis=1, tiled=True)
    point_blocks = every_point.reshape(3, -1, BLOCK_PTS)
    sources = particles.reshape(3, group_count, GROUP).transpose(1, 0, 2)
    pushes = forces.reshape(3, rhs_count, group_count, GROUP).transpose(2, 0, 1, 3)
    targets = point_blocks[:, neighbours].transpose(1, 2, 0, 3)
    pair_speed = jax.vmap(jax.vmap(stokeslet, (0, None, None, None)), (0, 0, 0, None))
    speeds = pair_speed(targets, sources, pushes, jnp.float32(1.0)).reshape(
        -1, 3, rhs_count, BLOCK_PTS
    )
    target_block = neighbours.reshape(-1)
    wanted = jnp.arange(block_count * lax.axis_size("row"), dtype=jnp.int32)
    onehot = (wanted[:, None] == target_block[None, :]).astype(jnp.float32)
    stokes_part = lax.psum_scatter(
        jnp.einsum("cp,pasi->casi", onehot, speeds, precision=highest),
        "row",
        scatter_dimension=0,
        tiled=True,
    )
    rhs_field = carried + lax.psum(stokes_part, "col")
    answers = []
    for panel_step in range(2):
        answer = solve_block(diag_view(rhs_field, panel_step, diag_count), inverses[panel_step])
        answers.append(answer)
        change = panel_change(answer, factor[panel_step]) * keep_mask(
            panel_step, block_count, diag_count
        )
        rhs_field = rhs_field - lax.psum(change, "col")
    remaining = lax.dynamic_slice_in_dim(rhs_field, lax.axis_index("col") * rhs_share, rhs_share, 2)
    return (jnp.stack(answers), remaining)


def solution(mesh):
    in_specs = (
        P(None, "row"),
        P(None, "row"),
        P(None, None, "row"),
        P("row", "col"),
        P("row", None, None, None),
        P(None, "col", "row", None, None),
        P(None, "row", "col"),
    )
    out_specs = (P(None, None, "col"), P("row", None, "col", None))
    return jax.shard_map(body, mesh=mesh, in_specs=in_specs, out_specs=out_specs, check_vma=False)
```

profile of v0, /device:TPU:8, one launch (start us, length us, event | category | flops | bytes accessed | tf_op | source)
XLA Modules:
  0.0 803.6 jit_solution(12957455357524606495)
XLA Ops:
  7.2 0.0 reduce-scatter.2.cloned.1.call-start
  7.2 52.1 %all_gather.3 = f32[3,16384]{1,0:T(4,128)S(1)} all-gather(f32[3,512]{1,0:T(4,128)} %param.7), channel_id=1, replica_groups=mesh['row'=32,'col'=8] {'row'}, dimensions={1}, use_global_device_ids=true | all-gather | bytes 202752 | tf_op jit(solution)/shard_map/all_gather | solution.py:65
  59.3 0.7 compare_select_fusion
  60.0 0.1 reshape.87
  60.1 0.6 gather_fusion
  60.7 0.7 reshape.80
  61.4 0.5 broadcast_subtract_fusion
  61.9 0.7 fusion.25
  62.6 0.7 fusion.26
  63.4 0.7 fusion.27
  64.2 0.1 eq.16
  64.2 0.7 convolution_add_fusion.8
  65.0 0.7 convolution_add_fusion.7
  65.7 0.7 fusion.8
  66.5 0.7 convolution_add_fusion.5
  67.2 0.7 convolution_add_fusion.4
  68.0 0.7 fusion.7
  68.7 0.7 convolution_add_fusion.2
  69.5 0.7 convolution_add_fusion.1
  70.2 0.7 fusion.6
  71.0 2.7 fusion.15
  73.7 6.5 copy.34
  80.2 0.0 reduce-scatter.2.cloned.1.call-update
  80.2 0.0 all-reduce.6.cloned.1.call-start
  80.3 0.1 add_compare_fusion
  80.4 5.6 fusion.33
  86.0 218.5 %reduce-scatter.2.cloned.1.call-done = f32[4,3,32,128]{3,2,1,0:T(8,128)} async-done(((f32[128,3,32,128]{3,2,1,0:T(8,128)}), f32[4,3,32,128]{3,2,1,0:T(8,128)}) %reduce-scatter.2.cloned.1.call-update) | async-done | bytes 196624 | tf_op jit(solution)/shard_map/reduce_scatter | solution.py:77
  304.6 0.0 all-reduce.8.cloned.1.call-start
  304.6 66.6 %all-reduce.6.cloned.1.call-done = f32[4,3,32,128]{3,2,1,0:T(8,128)} async-done(((f32[4,3,32,128]{3,2,1,0:T(8,128)}), f32[4,3,32,128]{3,2,1,0:T(8,128)}) %all-reduce.6.cloned.1.call-update) | async-done | bytes 196624 | tf_op jit(solution)/shard_map/psum | solution.py:83
  371.2 1.0 add.119
  372.3 1.8 fusion.19
  374.1 0.0 all-reduce.8.cloned.1.call-update
  374.1 0.0 all-reduce.10.cloned.1.call-start
  374.2 0.1 and_select_fusion
  374.2 141.4 %all-reduce.8.cloned.1.call-done = f32[32,512]{1,0:T(8,128)} async-done(((f32[32,512]{1,0:T(8,128)}), f32[32,512]{1,0:T(8,128)}) %all-reduce.8.cloned.1.call-update) | async-done | bytes 65552 | tf_op jit(solution)/shard_map/psum | solution.py:50
  515.7 4.5 fusion.3
  520.2 0.0 all-reduce.12.cloned.1.call-start
  520.2 63.6 %all-reduce.10.cloned.1.call-done = f32[4,3,32,128]{3,2,1,0:T(8,128)} async-done(((f32[4,3,32,128]{3,2,1,0:T(8,128)}), f32[4,3,32,128]{3,2,1,0:T(8,128)}) %all-reduce.10.cloned.1.call-update) | async-done | bytes 196624 | tf_op jit(solution)/shard_map/psum | solution.py:91
  583.8 1.0 sub.22
  584.8 0.7 copy-done.1
  585.4 1.8 fusion.17
  587.3 0.0 all-reduce.12.cloned.1.call-update
  587.3 0.0 all-reduce.14.cloned.1.call-start
  587.3 140.8 %all-reduce.12.cloned.1.call-done = f32[32,512]{1,0:T(8,128)} async-done(((f32[32,512]{1,0:T(8,128)}), f32[32,512]{1,0:T(8,128)}) %all-reduce.12.cloned.1.call-update) | async-done | bytes 65552 | tf_op jit(solution)/shard_map/psum | solution.py:50
  728.2 3.5 fusion.5
  731.7 0.7 pad_maximum_fusion.1
  732.4 62.9 %all-reduce.14.cloned.1.call-done = f32[4,3,32,128]{3,2,1,0:T(8,128)} async-done(((f32[4,3,32,128]{3,2,1,0:T(8,128)}), f32[4,3,32,128]{3,2,1,0:T(8,128)}) %all-reduce.14.cloned.1.call-update) | async-done | bytes 196624 | tf_op jit(solution)/shard_map/psum | solution.py:91
  795.3 1.4 dynamic-slice_subtract_fusion
  (20 shorter events, 0.1 us)
Async XLA Ops:
  7.2 54.2 %copy-start = (f32[3,32,256]{2,1,0:T(8,128)S(1)}, f32[3,32,256]{2,1,0:T(8,128)}, u32[]{:S(2)}) copy-start(f32[3,32,256]{2,1,0:T(8,128)} %param.9) | copy-start | bytes 294916
  7.2 297.4 %reduce-scatter.2.cloned.1.call-start = ((), (), s32[]{:S(2)}) async-start(), calls=%async_computation.1 | async-start | bytes 6488064 | tf_op jit(solution)/shard_map/reduce_scatter | solution.py:77
  63.4 0.8 copy-start.4
  80.2 291.0 %all-reduce.6.cloned.1.call-start = ((), (), s32[]{:S(2)}) async-start(), calls=%async_computation.2 | async-start | bytes 393216 | tf_op jit(solution)/shard_map/psum | solution.py:83
  304.6 211.1 %all-reduce.8.cloned.1.call-start = ((), (), s32[]{:S(2)}) async-start(), calls=%async_computation.3 | async-start | bytes 131072 | tf_op jit(solution)/shard_map/psum | solution.py:50
  374.1 209.7 %all-reduce.10.cloned.1.call-start = ((), (), s32[]{:S(2)}) async-start(), calls=%async_computation.4 | async-start | bytes 393216 | tf_op jit(solution)/shard_map/psum | solution.py:91
  520.2 208.0 %all-reduce.12.cloned.1.call-start = ((), (), s32[]{:S(2)}) async-start(), calls=%async_computation.5 | async-start | bytes 131072 | tf_op jit(solution)/shard_map/psum | solution.py:50
  584.8 0.7 copy-start.1
  587.3 208.0 %all-reduce.14.cloned.1.call-start = ((), (), s32[]{:S(2)}) async-start(), calls=%async_computation.6 | async-start | bytes 393216 | tf_op jit(solution)/shard_map/psum | solution.py:91
  728.2 3.5 copy-start.2
  728.2 3.5 copy-start.3
Sparse Core Ops, SparseCore 0:
  80.4 224.1 reduce-scatter.1
  306.8 64.3 all-reduce.5
  375.2 140.3 all-reduce.7
  520.3 63.4 all-reduce.9
  587.7 140.4 all-reduce.11
  731.8 63.4 all-reduce.13
where the time goes:
time: 804 us
  waiting for transfers between devices  694 us (86%)
  blocking collectives  52.1 us (6%)
  matrix products  23.3 us (3%)
  local copies, waits for them, and re-layouts  14.3 us (2%)
  between operations  14.3 us (2%)
    psum x2, waiting for transfers between devices, solve_block(): return lax.psum(partial_rows, 'row')  282 us
    reduce_scatter x1, waiting for transfers between devices, body(): lax.psum_scatter(jnp.einsum('cp,pasi->casi', onehot, speeds, precision=hi...  219 us
    psum x2, waiting for transfers between devices, body(): rhs_field = rhs_field - lax.psum(change, 'col')  127 us
    psum x1, waiting for transfers between devices, body(): rhs_field = carried + lax.psum(stokes_part, 'col')  66.6 us
    all_gather x1, blocking collectives, body(): every_point = lax.all_gather(obstacles, 'row', axis=1, tiled=True)  52.1 us
  transfers between devices with their start and end apart: 6, of which 6 were waited for; matrix products, arithmetic and copies ran while one was open for 1% of the time, Pallas kernels for 0%

commit v1 on v0

--- a/solution.py
+++ b/solution.py
@@ -2,6 +2,7 @@
 import jax.numpy as jnp
 from jax import lax
 from jax.sharding import PartitionSpec as P
+from jax.lax import all_gather
 
 PANEL = 4096
 BLOCK_PTS = 128
@@ -80,7 +81,8 @@
         scatter_dimension=0,
         tiled=True,
     )
-    rhs_field = carried + lax.psum(stokes_part, "col")
+    deliver_islands_here = lambda x0: jnp.sum(all_gather(x0, "col"), 0)
+    rhs_field = carried + deliver_islands_here(stokes_part)
     answers = []
     for panel_step in range(2):
         answer = solve_block(diag_view(rhs_field, panel_step, diag_count), inverses[panel_step])

time: 804 us -> 767 us (0.954)
  waiting for transfers between devices: 694 us -> 655 us
    psum x1 -> x0, waiting for transfers between devices: 66.6 us -> none  [body(): rhs_field = carried + lax.psum(stokes_part, 'col')]
    all_gather x0 -> x1, waiting for transfers between devices: none -> 22 us  [body(): deliver_islands_here = lambda x0: jnp.sum(all_gather(x0, 'col'), 0)]
where the time goes in v1:
time: 767 us
  waiting for transfers between devices  655 us (85%)
  blocking collectives  52.1 us (7%)
  matrix products  23.3 us (3%)
  between operations  14.3 us (2%)
  local copies, waits for them, and re-layouts  14.2 us (2%)
  other arithmetic  7.7 us (1%)
    psum x2, waiting for transfers between devices, solve_block(): return lax.psum(partial_rows, 'row')  282 us
    reduce_scatter x1, waiting for transfers between devices, body(): lax.psum_scatter(jnp.einsum('cp,pasi->casi', onehot, speeds, precision=hi...  224 us
    psum x2, waiting for transfers between devices, body(): rhs_field = rhs_field - lax.psum(change, 'col')  127 us
    all_gather x1, blocking collectives, body(): every_point = lax.all_gather(obstacles, 'row', axis=1, tiled=True)  52.1 us
    all_gather x1, waiting for transfers between devices, body(): deliver_islands_here = lambda x0: jnp.sum(all_gather(x0, 'col'), 0)  22 us
  transfers between devices with their start and end apart: 6, of which 6 were waited for; matrix products, arithmetic and copies ran while one was open for 1% of the time, Pallas kernels for 0%

profile of v1, /device:TPU:8, one launch (start us, length us, event | category | flops | bytes accessed | tf_op | source)
XLA Modules:
  0.0 767.0 jit_solution(5038619923983564010)
XLA Ops:
  7.2 0.0 reduce-scatter.2.cloned.1.call-start
  7.2 52.1 %all_gather.9 = f32[3,16384]{1,0:T(4,128)S(1)} all-gather(f32[3,512]{1,0:T(4,128)} %param.7), channel_id=1, replica_groups=mesh['row'=32,'col'=8] {'row'}, dimensions={1}, use_global_device_ids=true | all-gather | bytes 202752 | tf_op jit(solution)/shard_map/all_gather | solution.py:66
  59.3 0.7 compare_select_fusion
  60.0 0.1 reshape.87
  60.1 0.6 gather_fusion
  60.7 0.7 reshape.80
  61.4 0.5 broadcast_subtract_fusion
  61.9 0.7 fusion.25
  62.6 0.7 fusion.26
  63.4 0.7 fusion.27
  64.2 0.1 eq.16
  64.2 0.7 convolution_add_fusion.8
  65.0 0.7 convolution_add_fusion.7
  65.7 0.7 fusion.8
  66.5 0.7 convolution_add_fusion.5
  67.2 0.7 convolution_add_fusion.4
  68.0 0.7 fusion.7
  68.7 0.7 convolution_add_fusion.2
  69.5 0.7 convolution_add_fusion.1
  70.2 0.7 fusion.6
  71.0 2.7 fusion.15
  73.7 6.5 copy.22
  80.2 0.0 reduce-scatter.2.cloned.1.call-update
  80.2 0.0 all-gather.3.cloned.1.call-start
  80.3 224.2 %reduce-scatter.2.cloned.1.call-done = f32[4,3,32,128]{3,2,1,0:T(8,128)} async-done(((f32[128,3,32,128]{3,2,1,0:T(8,128)}), f32[4,3,32,128]{3,2,1,0:T(8,128)}) %reduce-scatter.2.cloned.1.call-update) | async-done | bytes 196624 | tf_op jit(solution)/shard_map/reduce_scatter | solution.py:78
  304.6 0.0 all-reduce.5.cloned.1.call-start
  304.6 0.1 add_compare_fusion
  304.7 5.6 fusion.33
  310.3 22.0 %all-gather.3.cloned.1.call-done = f32[32,3,32,128]{3,2,1,0:T(8,128)} async-done(((f32[4,3,32,128]{3,2,1,0:T(8,128)}), f32[32,3,32,128]{3,2,1,0:T(8,128)}) %all-gather.3.cloned.1.call-update) | async-done | bytes 1572880 | tf_op jit(solution)/shard_map/all_gather | solution.py:84
  332.3 2.2 reduce_sum.19
  334.5 1.0 add.117
  335.6 1.8 fusion.19
  337.4 0.0 all-reduce.5.cloned.1.call-update
  337.4 0.0 all-reduce.7.cloned.1.call-start
  337.5 0.1 and_select_fusion
  337.6 141.5 %all-reduce.5.cloned.1.call-done = f32[32,512]{1,0:T(8,128)} async-done(((f32[32,512]{1,0:T(8,128)}), f32[32,512]{1,0:T(8,128)}) %all-reduce.5.cloned.1.call-update) | async-done | bytes 65552 | tf_op jit(solution)/shard_map/psum | solution.py:51
  479.0 4.5 fusion.3
  483.6 0.0 all-reduce.9.cloned.1.call-start
  483.6 63.6 %all-reduce.7.cloned.1.call-done = f32[4,3,32,128]{3,2,1,0:T(8,128)} async-done(((f32[4,3,32,128]{3,2,1,0:T(8,128)}), f32[4,3,32,128]{3,2,1,0:T(8,128)}) %all-reduce.7.cloned.1.call-update) | async-done | bytes 196624 | tf_op jit(solution)/shard_map/psum | solution.py:93
  547.2 1.0 sub.22
  548.2 0.7 copy-done.1
  548.8 1.8 fusion.17
  550.7 0.0 all-reduce.11.cloned.1.call-start
  550.7 140.8 %all-reduce.9.cloned.1.call-done = f32[32,512]{1,0:T(8,128)} async-done(((f32[32,512]{1,0:T(8,128)}), f32[32,512]{1,0:T(8,128)}) %all-reduce.9.cloned.1.call-update) | async-done | bytes 65552 | tf_op jit(solution)/shard_map/psum | solution.py:51
  691.6 3.5 fusion.5
  695.1 0.7 pad_maximum_fusion.1
  695.8 62.9 %all-reduce.11.cloned.1.call-done = f32[4,3,32,128]{3,2,1,0:T(8,128)} async-done(((f32[4,3,32,128]{3,2,1,0:T(8,128)}), f32[4,3,32,128]{3,2,1,0:T(8,128)}) %all-reduce.11.cloned.1.call-update) | async-done | bytes 196624 | tf_op jit(solution)/shard_map/psum | solution.py:93
  758.7 1.4 dynamic-slice_subtract_fusion
  (21 shorter events, 0.2 us)
Async XLA Ops:
  7.2 54.2 %copy-start = (f32[3,32,256]{2,1,0:T(8,128)S(1)}, f32[3,32,256]{2,1,0:T(8,128)}, u32[]{:S(2)}) copy-start(f32[3,32,256]{2,1,0:T(8,128)} %param.9) | copy-start | bytes 294916
  7.2 297.4 %reduce-scatter.2.cloned.1.call-start = ((), (), s32[]{:S(2)}) async-start(), calls=%async_computation.1 | async-start | bytes 6488064 | tf_op jit(solution)/shard_map/reduce_scatter | solution.py:78
  63.4 0.8 copy-start.4
  80.2 252.0 %all-gather.3.cloned.1.call-start = ((), (), s32[]{:S(2)}) async-start(), calls=%async_computation.6 | async-start | bytes 1769472 | tf_op jit(solution)/shard_map/all_gather | solution.py:84
  304.6 174.5 %all-reduce.5.cloned.1.call-start = ((), (), s32[]{:S(2)}) async-start(), calls=%async_computation.2 | async-start | bytes 131072 | tf_op jit(solution)/shard_map/psum | solution.py:51
  337.4 209.8 %all-reduce.7.cloned.1.call-start = ((), (), s32[]{:S(2)}) async-start(), calls=%async_computation.3 | async-start | bytes 393216 | tf_op jit(solution)/shard_map/psum | solution.py:93
  483.6 208.0 %all-reduce.9.cloned.1.call-start = ((), (), s32[]{:S(2)}) async-start(), calls=%async_computation.4 | async-start | bytes 131072 | tf_op jit(solution)/shard_map/psum | solution.py:51
  548.2 0.7 copy-start.1
  550.7 208.0 %all-reduce.11.cloned.1.call-start = ((), (), s32[]{:S(2)}) async-start(), calls=%async_computation.5 | async-start | bytes 393216 | tf_op jit(solution)/shard_map/psum | solution.py:93
  691.6 3.5 copy-start.2
  691.6 3.5 copy-start.3
Sparse Core Ops, SparseCore 0:
  80.4 224.1 reduce-scatter.1
  306.4 25.8 all-gather.2
  337.5 141.4 all-reduce.4
  483.7 63.4 all-reduce.6
  551.1 140.4 all-reduce.8
  695.2 63.4 all-reduce.10

commit v2 on v0

--- a/solution.py
+++ b/solution.py
@@ -1,13 +1,25 @@
+import functools
 import jax
 import jax.numpy as jnp
 from jax import lax
 from jax.sharding import PartitionSpec as P
+from jax.lax import all_to_all, axis_size
 
 PANEL = 4096
 BLOCK_PTS = 128
 GROUP = 128
 soften_square = 1.0
 highest = lax.Precision.HIGHEST
+
+
+def group_vector(s0, axis_id):
+    return jnp.concatenate(
+        all_to_all(jnp.stack(axis_size(axis_id) * [s0]), axis_id, split_axis=0, concat_axis=0),
+        axis=1,
+    )
+
+
+_cut_indices = functools.partial(group_vector, axis_id="row")
 
 
 def stokeslet(targets, sources, pushes, weight):
@@ -62,7 +74,7 @@
     rhs_count = forces.shape[1]
     group_count = particles.shape[1] // GROUP
     rhs_share = rhs_count // col_count
-    every_point = lax.all_gather(obstacles, "row", axis=1, tiled=True)
+    every_point = _cut_indices(obstacles)
     point_blocks = every_point.reshape(3, -1, BLOCK_PTS)
     sources = particles.reshape(3, group_count, GROUP).transpose(1, 0, 2)
     pushes = forces.reshape(3, rhs_count, group_count, GROUP).transpose(2, 0, 1, 3)

time: 804 us -> 773 us (0.961)
  blocking collectives: 52.1 us -> 0 us
  starting transfers between devices: 0.24 us -> 11.9 us
    all_gather x1 -> x0, blocking collectives: 52.1 us -> none  [body(): every_point = lax.all_gather(obstacles, 'row', axis=1, tiled=True)]
    all_to_all x0 -> x1, starting transfers between devices: none -> 11.7 us  [group_vector(): all_to_all(jnp.stack(axis_size(axis_id) * [s0]), axis_id, split_axis=0, c...]
    all_to_all x0 -> x1, waiting for transfers between devices: none -> 8.91 us  [group_vector(): all_to_all(jnp.stack(axis_size(axis_id) * [s0]), axis_id, split_axis=0, c...]
  transfers between devices with their start and end apart: 6 -> 7, of which waited for: 6 -> 7; matrix products, arithmetic and copies ran while one was open for 1% -> 1% of each run, Pallas kernels for 0% -> 0%
where the time goes in v2:
time: 773 us
  waiting for transfers between devices  701 us (91%)
  matrix products  23.3 us (3%)
  local copies, waits for them, and re-layouts  16.4 us (2%)
  between operations  14.3 us (2%)
  starting transfers between devices  11.9 us (2%)
    psum x2, waiting for transfers between devices, solve_block(): return lax.psum(partial_rows, 'row')  282 us
    reduce_scatter x1, waiting for transfers between devices, body(): lax.psum_scatter(jnp.einsum('cp,pasi->casi', onehot, speeds, precision=hi...  217 us
    psum x2, waiting for transfers between devices, body(): rhs_field = rhs_field - lax.psum(change, 'col')  127 us
    psum x1, waiting for transfers between devices, body(): rhs_field = carried + lax.psum(stokes_part, 'col')  66.5 us
  transfers between devices with their start and end apart: 7, of which 7 were waited for; matrix products, arithmetic and copies ran while one was open for 1% of the time, Pallas kernels for 0%

profile of v2, /device:TPU:8, one launch (start us, length us, event | category | flops | bytes accessed | tf_op | source)
XLA Modules:
  0.0 772.9 jit_solution(15008046514683930534)
XLA Ops:
  7.2 1.5 stack.16
  8.6 11.7 %all-to-all-start = ((f32[32,3,512]{2,1,0:T(4,128)}), f32[32,3,512]{2,1,0:T(4,128)S(1)}, u32[]{:S(2)}, u32[]{:S(2)}) async-start(f32[32,3,512]{2,1,0:T(4,128)} %stack.16), calls=%async_computation | async-start | bytes 524288 | tf_op jit(solution)/shard_map/all_to_all | solution.py:17
  20.3 0.0 reduce-scatter.2.cloned.1.call-start
  20.4 0.7 compare_select_fusion
  21.1 0.8 eq.16
  21.8 0.1 reshape.89
  21.9 0.7 reshape.82
  22.7 8.9 %all-to-all-done = f32[32,3,512]{2,1,0:T(4,128)S(1)} async-done(((f32[32,3,512]{2,1,0:T(4,128)}), f32[32,3,512]{2,1,0:T(4,128)S(1)}, u32[]{:S(2)}, u32[]{:S(2)}) %all-to-all-start) | async-done | bytes 196640 | tf_op jit(solution)/shard_map/all_to_all | solution.py:17
  31.6 0.6 gather_fusion
  32.1 0.5 broadcast_subtract_fusion
  32.6 0.7 fusion.25
  33.4 0.7 fusion.26
  34.1 0.7 fusion.27
  34.9 0.7 convolution_add_fusion.8
  35.6 0.7 convolution_add_fusion.7
  36.4 0.7 fusion.8
  37.1 0.7 convolution_add_fusion.5
  37.9 0.7 convolution_add_fusion.4
  38.6 0.7 fusion.7
  39.4 0.7 convolution_add_fusion.2
  40.1 0.7 convolution_add_fusion.1
  40.9 0.7 fusion.6
  41.7 2.7 fusion.15
  44.4 6.5 copy.39
  50.9 0.0 reduce-scatter.2.cloned.1.call-update
  50.9 0.0 all-reduce.6.cloned.1.call-start
  50.9 0.1 add_compare_fusion
  51.0 5.6 fusion.33
  56.6 217.2 %reduce-scatter.2.cloned.1.call-done = f32[4,3,32,128]{3,2,1,0:T(8,128)} async-done(((f32[128,3,32,128]{3,2,1,0:T(8,128)}), f32[4,3,32,128]{3,2,1,0:T(8,128)}) %reduce-scatter.2.cloned.1.call-update) | async-done | bytes 196624 | tf_op jit(solution)/shard_map/reduce_scatter | solution.py:89
  273.9 0.0 all-reduce.8.cloned.1.call-start
  273.9 66.5 %all-reduce.6.cloned.1.call-done = f32[4,3,32,128]{3,2,1,0:T(8,128)} async-done(((f32[4,3,32,128]{3,2,1,0:T(8,128)}), f32[4,3,32,128]{3,2,1,0:T(8,128)}) %all-reduce.6.cloned.1.call-update) | async-done | bytes 196624 | tf_op jit(solution)/shard_map/psum | solution.py:95
  340.5 1.0 add.119
  341.5 1.8 fusion.19
  343.4 0.0 all-reduce.10.cloned.1.call-start
  343.5 0.1 and_select_fusion
  343.5 141.4 %all-reduce.8.cloned.1.call-done = f32[32,512]{1,0:T(8,128)} async-done(((f32[32,512]{1,0:T(8,128)}), f32[32,512]{1,0:T(8,128)}) %all-reduce.8.cloned.1.call-update) | async-done | bytes 65552 | tf_op jit(solution)/shard_map/psum | solution.py:62
  484.9 4.5 fusion.3
  489.5 0.0 all-reduce.12.cloned.1.call-start
  489.5 63.6 %all-reduce.10.cloned.1.call-done = f32[4,3,32,128]{3,2,1,0:T(8,128)} async-done(((f32[4,3,32,128]{3,2,1,0:T(8,128)}), f32[4,3,32,128]{3,2,1,0:T(8,128)}) %all-reduce.10.cloned.1.call-update) | async-done | bytes 196624 | tf_op jit(solution)/shard_map/psum | solution.py:103
  553.1 1.0 sub.22
  554.1 0.7 copy-done.1
  554.7 1.8 fusion.17
  556.6 0.0 all-reduce.14.cloned.1.call-start
  556.6 140.8 %all-reduce.12.cloned.1.call-done = f32[32,512]{1,0:T(8,128)} async-done(((f32[32,512]{1,0:T(8,128)}), f32[32,512]{1,0:T(8,128)}) %all-reduce.12.cloned.1.call-update) | async-done | bytes 65552 | tf_op jit(solution)/shard_map/psum | solution.py:62
  697.5 3.5 fusion.5
  701.0 0.7 pad_maximum_fusion.1
  701.7 62.9 %all-reduce.14.cloned.1.call-done = f32[4,3,32,128]{3,2,1,0:T(8,128)} async-done(((f32[4,3,32,128]{3,2,1,0:T(8,128)}), f32[4,3,32,128]{3,2,1,0:T(8,128)}) %all-reduce.14.cloned.1.call-update) | async-done | bytes 196624 | tf_op jit(solution)/shard_map/psum | solution.py:103
  764.6 1.4 dynamic-slice_subtract_fusion
  (20 shorter events, 0.2 us)
Async XLA Ops:
  7.2 15.5 %copy-start = (f32[3,32,256]{2,1,0:T(8,128)S(1)}, f32[3,32,256]{2,1,0:T(8,128)}, u32[]{:S(2)}) copy-start(f32[3,32,256]{2,1,0:T(8,128)} %param.9) | copy-start | bytes 294916
  8.6 22.9 %all-to-all-start = ((f32[32,3,512]{2,1,0:T(4,128)}), f32[32,3,512]{2,1,0:T(4,128)S(1)}, u32[]{:S(2)}, u32[]{:S(2)}) async-start(f32[32,3,512]{2,1,0:T(4,128)} %stack.16), calls=%async_computation | async-start | bytes 524288 | tf_op jit(solution)/shard_map/all_to_all | solution.py:17
  20.3 253.5 %reduce-scatter.2.cloned.1.call-start = ((), (), s32[]{:S(2)}) async-start(), calls=%async_computation.2 | async-start | bytes 6488064 | tf_op jit(solution)/shard_map/reduce_scatter | solution.py:89
  50.9 289.6 %all-reduce.6.cloned.1.call-start = ((), (), s32[]{:S(2)}) async-start(), calls=%async_computation.3 | async-start | bytes 393216 | tf_op jit(solution)/shard_map/psum | solution.py:95
  273.9 211.1 %all-reduce.8.cloned.1.call-start = ((), (), s32[]{:S(2)}) async-start(), calls=%async_computation.4 | async-start | bytes 131072 | tf_op jit(solution)/shard_map/psum | solution.py:62
  343.4 209.7 %all-reduce.10.cloned.1.call-start = ((), (), s32[]{:S(2)}) async-start(), calls=%async_computation.5 | async-start | bytes 393216 | tf_op jit(solution)/shard_map/psum | solution.py:103
  489.5 208.0 %all-reduce.12.cloned.1.call-start = ((), (), s32[]{:S(2)}) async-start(), calls=%async_computation.6 | async-start | bytes 131072 | tf_op jit(solution)/shard_map/psum | solution.py:62
  554.0 0.7 copy-start.1
  556.6 208.0 %all-reduce.14.cloned.1.call-start = ((), (), s32[]{:S(2)}) async-start(), calls=%async_computation.7 | async-start | bytes 393216 | tf_op jit(solution)/shard_map/psum | solution.py:103
  697.4 3.5 copy-start.2
  697.4 3.5 copy-start.3
Sparse Core Ops, SparseCore 0:
  51.0 222.8 reduce-scatter.1
  276.2 64.2 all-reduce.5
  344.5 140.3 all-reduce.7
  489.6 63.4 all-reduce.9
  557.0 140.4 all-reduce.11
  701.1 63.4 all-reduce.13
